TPU v7x, 128 devices: a whole 4x4x4 slice. The times are simulated.
128 devices in a mesh: req: 32 (over x, y, core), mlp: 4 (over z).
Axes of the slice: x: 4, y: 4, z: 4, core: 2. Of those that a mesh axis runs over, the one named last changes fastest.
Arguments:
- hidden_in: bfloat16 [64, 512, 2048], P('req'), may hold values from -6 to 6
- lengths: int32 [64], replicated, may hold values from 1 to 512, 16384 in all
- slot_request: int32 [64], replicated, may hold values from 0 to 63, each once
- adapter_of: int32 [64], replicated, may hold values from 0 to 63, as said below
- adapter_slot: int32 [64], replicated, may hold values from 0 to 63, each once
- norm_gain_attn: float32 [2048], replicated, may hold values from 0.5 to 1.5
- norm_gain_mlp: float32 [2048], replicated, may hold values from 0.5 to 1.5
- final_gain: float32 [2048], replicated, may hold values from 0.5 to 1.5
- w_qkv: bfloat16 [2048, 3, 2048], P(None, None, 'mlp')
- w_out: bfloat16 [2048, 2048], P('mlp'), may hold values from -0.125 to 0.125
- w_gateup: bfloat16 [2048, 2, 4096], P('req', None, 'mlp'), may hold values from -0.125 to 0.125
- w_down: bfloat16 [4096, 2048], P('mlp', 'req'), may hold values from -0.09375 to 0.09375
- adapter_down: bfloat16 [64, 16, 2048], P('req'), may hold values from -0.125 to 0.125
- adapter_up: bfloat16 [64, 16, 2048], P('req', None, 'mlp'), may hold values from -1.5 to 1.5
- vocab: bfloat16 [49152, 2048], P(('req', 'mlp')), may hold values from -0.375 to 0.375
Outputs:
- out_hidden: bfloat16 [64, 512, 2048], P('req')
- request_norm: float32 [64], replicated
- request_peak: float32 [64], replicated
Inputs may be any that keep to these rules, and one draw needn't show every extreme that they name: Some request has exactly 512 tokens, and all lengths together sum to 16384. `slot_request`: each request sits in exactly one slot. `adapter_of`: exactly 16 distinct adapters are named. `adapter_slot`: each adapter sits in exactly one row of the adapter tables.
All inputs are finite; a program needn't handle non-finite values.
Results may differ from a plain program's by a relative error of at most 0.018.
Values may be sent and summed in bfloat16 or wider, within the bound.
A program may use at most 128 MiB of HBM per device.

v0:
```python
import jax
import jax.numpy as jnp
from jax import lax
from jax.sharding import PartitionSpec as P

HEAD_WIDTH = 64
EPSILON = 1e-05
ROPE_BASE = 130000.0
ADAPTER_SCALE = 2.0
MASKED = -1e30


def rms_norm(values, gain):
    return values * lax.rsqrt(jnp.mean(values * values, axis=-1, keepdims=True) + EPSILON) * gain


def rotary_embedded(tensor):
    length = tensor.shape[-3]
    half_width = tensor.shape[-1] // 2
    frequency = ROPE_BASE ** (-(jnp.arange(half_width, dtype=jnp.float32) * 2.0 / tensor.shape[-1]))
    angles = jnp.arange(length, dtype=jnp.float32)[:, None] * frequency[None, :]
    cosine = jnp.cos(angles)[:, None, :]
    sine_part = jnp.sin(angles)[:, None, :]
    front_half = tensor[..., :half_width]
    back_half = tensor[..., half_width:]
    return jnp.concatenate(
        [front_half * cosine - back_half * sine_part, back_half * cosine + front_half * sine_part],
        axis=-1,
    )


def per_device(
    hidden_in,
    lengths,
    slot_request,
    adapter_of,
    adapter_slot,
    norm_gain_attn,
    norm_gain_mlp,
    final_gain,
    w_qkv,
    w_out,
    w_gateup,
    w_down,
    adapter_down,
    adapter_up,
    vocab,
):
    req_index = lax.axis_index("req")
    slots_number, sequence_length, width = hidden_in.shape
    row_count = slots_number * sequence_length
    head_cols = w_qkv.shape[2]
    heads_number = head_cols // HEAD_WIDTH
    unit_cols = w_gateup.shape[2]
    requests = lax.dynamic_slice_in_dim(slot_request, req_index * slots_number, slots_number)
    own_lengths = jnp.take(lengths, requests)
    own_adapters = jnp.take(adapter_of, requests)
    table_rows = jnp.take(adapter_slot, own_adapters)
    positions = jnp.arange(sequence_length, dtype=jnp.int32)
    residual_in = hidden_in.astype(jnp.float32)
    normed = rms_norm(residual_in, norm_gain_attn).astype(jnp.bfloat16)
    projected_rows = jnp.dot(
        normed.reshape(row_count, width),
        w_qkv.reshape(width, 3 * head_cols),
        preferred_element_type=jnp.float32,
    ).reshape(slots_number, sequence_length, 3, head_cols)
    down_all, up_all = (
        lax.all_gather(adapter_down, "req", axis=0, tiled=True),
        lax.all_gather(adapter_up, "req", axis=0, tiled=True),
    )
    down_rows = jnp.take(down_all, table_rows, axis=0)
    up_rows = jnp.take(up_all, table_rows, axis=0)
    low_rank = jnp.einsum(
        "bsd,brd->bsr", normed, down_rows, preferred_element_type=jnp.float32
    ).astype(jnp.bfloat16)
    raised_rows = jnp.einsum("bsr,brc->bsc", low_rank, up_rows, preferred_element_type=jnp.float32)
    queries = rotary_embedded(
        (projected_rows[:, :, 0] + ADAPTER_SCALE * raised_rows).reshape(
            slots_number, sequence_length, heads_number, HEAD_WIDTH
        )
    ).astype(jnp.bfloat16)
    key_heads = rotary_embedded(
        projected_rows[:, :, 1].reshape(slots_number, sequence_length, heads_number, HEAD_WIDTH)
    ).astype(jnp.bfloat16)
    value_heads = (
        projected_rows[:, :, 2]
        .reshape(slots_number, sequence_length, heads_number, HEAD_WIDTH)
        .astype(jnp.bfloat16)
    )
    causal = positions[None, :] <= positions[:, None]

    def attend(slot_items):
        query_one, key_one, value_one, length = slot_items
        scores = jnp.einsum(
            "qhd,khd->hqk", query_one, key_one, preferred_element_type=jnp.float32
        ) * HEAD_WIDTH ** (-0.5)
        allowed = causal & (positions[None, :] < length)
        scores = jnp.where(allowed[None], scores, MASKED)
        probabilities = jax.nn.softmax(scores, axis=-1).astype(jnp.bfloat16)
        return jnp.einsum(
            "hqk,khd->qhd", probabilities, value_one, preferred_element_type=jnp.float32
        ).astype(jnp.bfloat16)

    attended = lax.map(attend, (queries, key_heads, value_heads, own_lengths))
    head_part = jnp.dot(
        attended.reshape(row_count, head_cols), w_out, preferred_element_type=jnp.float32
    )
    mixed_heads = lax.psum(head_part.astype(jnp.bfloat16), "mlp").astype(jnp.float32)
    stream = (residual_in + mixed_heads.reshape(slots_number, sequence_length, width)).astype(
        jnp.bfloat16
    )
    normed_mid = (
        rms_norm(stream.astype(jnp.float32), norm_gain_mlp)
        .astype(jnp.bfloat16)
        .reshape(row_count, width)
    )
    shard_piece = lax.all_gather(w_gateup, "req", axis=0, tiled=True)
    gate_up = jnp.dot(
        normed_mid,
        shard_piece.reshape(shard_piece.shape[0], 2 * unit_cols),
        preferred_element_type=jnp.float32,
    )
    activated = (jax.nn.silu(gate_up[:, :unit_cols]) * gate_up[:, unit_cols:]).astype(jnp.bfloat16)
    unit_part = jnp.dot(
        activated,
        lax.all_gather(w_down, "req", axis=1, tiled=True),
        preferred_element_type=jnp.float32,
    )
    unit_total = lax.psum(unit_part.astype(jnp.bfloat16), "mlp").astype(jnp.float32)
    result = stream.astype(jnp.float32) + unit_total.reshape(slots_number, sequence_length, width)
    live = positions[None, :] < own_lengths[:, None]
    out_hidden = jnp.where(live[:, :, None], result, 0.0).astype(jnp.bfloat16)
    out_float = out_hidden.astype(jnp.float32)
    square_sum = jnp.sum(out_float * out_float, axis=(1, 2))
    slot_norm = jnp.sqrt(square_sum / (own_lengths.astype(jnp.float32) * width))
    picked = (positions[None, :] == own_lengths[:, None] - 1).astype(jnp.float32)
    last_rows = jnp.einsum("bs,bsd->bd", picked, out_float, precision=lax.Precision.HIGHEST)
    last_rounded = lax.optimization_barrier(rms_norm(last_rows, final_gain).astype(jnp.bfloat16))
    last_normed = last_rounded.astype(jnp.float32)
    every_last, every_norm = (
        lax.all_gather(last_normed, "req", axis=0, tiled=True),
        lax.all_gather(slot_norm, "req", axis=0, tiled=True),
    )
    logits = lax.dot_general(
        every_last.astype(jnp.bfloat16),
        vocab,
        (((1,), (1,)), ((), ())),
        preferred_element_type=jnp.float32,
    )
    slot_peak = lax.pmax(jnp.max(logits, axis=1), ("req", "mlp"))
    request_total = slot_request.shape[0]
    owners = slot_request[None, :] == jnp.arange(request_total, dtype=jnp.int32)[:, None]
    request_norm = jnp.sum(jnp.where(owners, every_norm[None, :], 0.0), axis=1)
    request_peak = jnp.sum(jnp.where(owners, slot_peak[None, :], 0.0), axis=1)
    return (out_hidden, request_norm, request_peak)


def solution(mesh):
    return jax.shard_map(
        per_device,
        mesh=mesh,
        in_specs=(
            P("req", None, None),
            P(),
            P(),
            P(),
            P(),
            P(),
            P(),
            P(),
            P(None, None, "mlp"),
            P("mlp", None),
            P("req", None, "mlp"),
            P("mlp", "req"),
            P("req", None, None),
            P("req", None, "mlp"),
            P(("req", "mlp"), None),
        ),
        out_specs=(P("req", None, None), P(), P()),
        check_vma=False,
    )
```

profile of v0, /device:TPU:0, one launch (start us, length us, event | category | flops | bytes accessed | tf_op | source)
XLA Modules:
  0.0 623.8 jit_solution(15625885839021791205)
XLA Ops:
  7.2 0.7 all-gather.8.cloned.1.call-update
  8.0 0.7 all-gather.6.cloned.1.call-update
  8.7 8.8 %copy.26 = bf16[2048,3,512]{0,2,1:T(8,128)(2,1)} copy(bf16[2048,3,512]{2,0,1:T(8,128)(2,1)} %param.27) | data formatting | bytes 12582912 | tf_op args[8]
  17.5 3.2 fusion.44
  20.8 0.2 copy-done.4
  21.0 9.1 %fusion.53 = f32[2,512,3,512]{1,3,2,0:T(8,128)S(1)} fusion(bf16[2048,3,512]{0,2,1:T(8,128)(2,1)} %copy.26, bf16[2,512,2048]{2,1,0:T(8,128)(2,1)S(1)} %copy-done.4, f32[2048]{0:T(1024)S(1)} %copy-done.13, f32[2,512]{1,0:T(2,128)S(1)} %add_rsqrt_fusion.1), kind=kOutput, calls=%fused_computation.55 | convolution fusion | flops 6450839552 | bytes 16789504 | tf_op jit(solution)/shard_map/dot_general | solution.py:62
  30.1 1.7 slice.51
  31.8 1.6 copy-done.9
  33.3 0.1 slice.74
  33.5 0.1 compare_select_fusion.1
  33.6 0.6 gather_fusion.2
  34.2 0.6 gather_fusion.3
  34.9 0.1 broadcast_add_fusion
  35.0 0.6 gather_fusion.4
  35.6 0.3 fusion.73
  36.0 19.5 %all-gather.8.cloned.1.call-done = bf16[64,16,512]{2,1,0:T(8,128)(2,1)} async-done(((bf16[2,16,512]{2,1,0:T(8,128)(2,1)}), bf16[64,16,512]{2,1,0:T(8,128)(2,1)}) %all-gather.8.cloned.1.call-update) | async-done | bytes 1048592 | tf_op jit(solution)/shard_map/all_gather | solution.py:69
  55.4 1.8 gather_fusion.1
  57.2 45.8 %all-gather.6.cloned.1.call-done = bf16[64,16,2048]{2,1,0:T(8,128)(2,1)} async-done(((bf16[2,16,2048]{2,1,0:T(8,128)(2,1)}), bf16[64,16,2048]{2,1,0:T(8,128)(2,1)}) %all-gather.6.cloned.1.call-update) | async-done | bytes 4194320 | tf_op jit(solution)/shard_map/all_gather | solution.py:68
  103.0 2.7 gather_fusion
  105.8 5.8 fusion.61
  111.6 2.9 subtract_convert_fusion
  114.4 1.5 pad_maximum_fusion
  116.0 28.0 %while.11 = (s32[]{:T(128)}, bf16[2,512,8,64]{1,3,2,0:T(8,128)(2,1)}, bf16[2,512,8,64]{1,3,2,0:T(8,128)(2,1)S(1)}, s32[2]{0:T(128)S(1)}, bf16[2,512,8,64]{1,3,2,...) while((s32[]{:T(128)}, bf16[2,512,8,64]{1,3,2,0:T(8,128)(2,1)}, ...), condition=%wide.region_4.6_spmd.clone, body=%wide.region_1.5_spmd.clone.sunk | while | flops 550241280 | bytes 19434588 | solution.py:104
  116.0 0.6 dynamic_slice.68
  116.6 0.6 iota_compare_fusion.5
  117.2 0.1 fusion.115
  117.3 7.6 %fusion.116 = (f32[8,512]{1,0:T(8,128)S(1)}, f32[8,512,512]{1,2,0:T(8,128)}) fusion(pred[512,512]{0,1:T(8,128)(4,1)S(1)} %fusion.115, bf16[2,512,8,64]{1,3,2,0:T(8,128)(2,1)} %get-tuple-element.155, s32[]{:T(128)} %get-tuple-element.143, bf16[2,512,8,64]{1,3,2,0:T(8,128)(2,1)} %get-tuple-element.154), kind=kOutput, calls=%fused_computation.116.clone.1 | convolution fusion | flops 276824576 | bytes 9716736 | tf_op jit(solution)/shard_map/while/body/eval_jaxpr/sub | solution.py:99
  124.9 5.0 fusion.117
  130.0 0.6 dynamic_slice.68
  130.5 0.6 iota_compare_fusion.5
  131.2 0.1 fusion.115
  131.3 7.6 %fusion.116 = (f32[8,512]{1,0:T(8,128)S(1)}, f32[8,512,512]{1,2,0:T(8,128)}) fusion(pred[512,512]{0,1:T(8,128)(4,1)S(1)} %fusion.115, bf16[2,512,8,64]{1,3,2,0:T(8,128)(2,1)} %get-tuple-element.155, s32[]{:T(128)} %get-tuple-element.143, bf16[2,512,8,64]{1,3,2,0:T(8,128)(2,1)} %get-tuple-element.154), kind=kOutput, calls=%fused_computation.116.clone.1 | convolution fusion | flops 276824576 | bytes 9716736 | tf_op jit(solution)/shard_map/while/body/eval_jaxpr/sub | solution.py:99
  138.9 5.0 fusion.117
  143.9 2.3 copy.27
  146.3 0.2 copy.32
  146.5 4.4 convolution_convert_fusion
  151.0 0.5 all-gather.10.cloned.1.call-update
  151.6 0.5 all-gather.12.cloned.1.call-update
  152.2 91.4 %all-reduce.4.cloned.1.call-done = bf16[2,512,2048]{2,1,0:T(8,128)(2,1)} async-done(((bf16[2,512,2048]{2,1,0:T(8,128)(2,1)}), bf16[2,512,2048]{2,1,0:T(8,128)(2,1)}) %all-reduce.4.cloned.1.call-update) | async-done | bytes 4194320 | tf_op jit(solution)/shard_map/psum | solution.py:108
  243.6 5.0 fusion.48
  248.7 0.9 copy-done.6
  249.5 3.6 fusion.50
  253.1 45.4 %all-gather.10.cloned.1.call-done = bf16[2048,2,1024]{2,1,0:T(2,128)(2,1)} async-done(((bf16[64,2,1024]{2,1,0:T(2,128)(2,1)}), bf16[2048,2,1024]{2,1,0:T(2,128)(2,1)}) %all-gather.10.cloned.1.call-update) | async-done | bytes 8388624 | tf_op jit(solution)/shard_map/all_gather | solution.py:117
  298.5 10.3 %copy.33 = bf16[256,8,2,1024]{3,1,2,0:T(8,128)(2,1)} copy(bf16[256,8,2,1024]{3,2,1,0:T(2,128)(2,1)} %bitcast.100) | data formatting | bytes 16777216
  308.8 13.3 %fusion.97 = f32[1024,2048]{1,0:T(8,128)} fusion(bf16[1024,2048]{1,0:T(8,128)(2,1)S(1)} %bitcast.102, bf16[2048,2048]{1,0:T(8,128)(2,1)} %bitcast.101), kind=kOutput, calls=%fused_computation.117 | convolution fusion | flops 8589934592 | bytes 20971520 | tf_op jit(solution)/shard_map/dot_general | solution.py:118
  322.0 24.4 %all-gather.12.cloned.1.call-done = bf16[1024,2048]{0,1:T(8,128)(2,1)} async-done(((bf16[1024,64]{0,1:T(8,128)(2,1)}), bf16[1024,2048]{0,1:T(8,128)(2,1)}) %all-gather.12.cloned.1.call-update) | async-done | bytes 4194320 | tf_op jit(solution)/shard_map/all_gather | solution.py:126
  346.4 11.2 %convolution_convert_fusion.1 = bf16[1024,2048]{1,0:T(8,128)(2,1)} fusion(bf16[1024,2048]{0,1:T(8,128)(2,1)} %all-gather.12.cloned.1.call-done, f32[1024,2048]{1,0:T(8,128)} %fusion.97), kind=kOutput, calls=%fused_computation.61 | convolution fusion | flops 4303355904 | bytes 16777216 | tf_op jit(solution)/shard_map/dot_general | solution.py:124
  357.7 0.6 copy-done.14
  358.3 0.6 dynamic-slice
  359.5 0.1 iota_compare_fusion.3
  359.6 0.1 compare_bitcast_fusion
  359.7 90.6 %all-reduce.6.cloned.1.call-done = bf16[2,512,2048]{2,1,0:T(8,128)(2,1)} async-done(((bf16[2,512,2048]{2,1,0:T(8,128)(2,1)}), bf16[2,512,2048]{2,1,0:T(8,128)(2,1)}) %all-reduce.6.cloned.1.call-update) | async-done | bytes 4194320 | tf_op jit(solution)/shard_map/psum | solution.py:129
  450.3 6.9 %multiply_reduce_fusion = (f32[2]{0:T(128)S(1)}, bf16[2,512,2048]{2,1,0:T(8,128)(2,1)S(1)}) fusion(bf16[2,512,2048]{2,1,0:T(8,128)(2,1)} %all-reduce.6.cloned.1.call-done, bf16[2,512,2048]{2,1,0:T(8,128)(2,1)} %all-reduce.4.cloned.1.call-done, bf16[2,512,2048]{2,1,0:T(8,128)(2,1)} %param.19, pred[2,512]{1,0:T(4,128)(4,1)S(1)} %iota_compare_fusion.3), kind=kLoop, calls=%fused_computation.54 | loop fusion | flops 25165822 | bytes 16778248 | tf_op jit(solution)/shard_map/reduce_sum | solution.py:134
  457.3 2.0 copy-done.7
  459.3 0.7 fusion.82
  459.9 0.1 fusion.78
  460.1 0.1 fusion.80
  460.2 24.8 %all-gather = bf16[32,2,2048]{2,1,0:T(2,128)(2,1)S(1)} all-gather(bf16[1,2,2048]{2,1,0:T(2,128)(2,1)S(1)} %bitcast.109), channel_id=1, replica_groups=mesh['req'=32,'mlp'=4] {'req'}, dimensions={0}, use_global_device_ids=true | all-gather | bytes 270336 | tf_op jit(solution)/shard_map/all_gather | solution.py:141
  484.9 0.1 reshape.230
  485.0 2.1 convolution_reduce_fusion
  487.2 64.5 %pmax.7 = f32[64]{0:T(128)S(1)} all-reduce(f32[64]{0:T(128)S(1)} %convolution_reduce_fusion), channel_id=1, replica_groups=mesh['req'=32,'mlp'=4] {'req','mlp'}, use_global_device_ids=true, to_apply=%region_12.14 | all-reduce | flops 64 | bytes 512 | tf_op jit(solution)/shard_map/pmax | solution.py:150
  551.6 0.1 sqrt_dynamic-update-slice_fusion
  551.7 64.6 %all-reduce = f32[64]{0:T(128)S(1)} all-reduce(f32[64]{0:T(128)S(1)} %sqrt_dynamic-update-slice_fusion), channel_id=1, replica_groups=mesh['req'=32,'mlp'=4] {'req'}, use_global_device_ids=true, to_apply=%add | all-reduce | flops 64 | bytes 512
  616.3 0.6 select_reduce_fusion
  (43 shorter events, 0.4 us)
Async XLA Ops:
  7.2 139.3 %copy-start = (bf16[512,2048]{1,0:T(8,128)(2,1)S(1)}, bf16[512,2048]{1,0:T(8,128)(2,1)}, u32[]{:S(2)}) copy-start(bf16[512,2048]{1,0:T(8,128)(2,1)} %param.28) | copy-start | bytes 6291460
  7.2 48.2 %all-gather.8.cloned.1.call-start = ((), (), s32[]{:S(2)}) async-start(), calls=%async_computation.1 | async-start | bytes 1081344 | tf_op jit(solution)/shard_map/all_gather | solution.py:69
  7.9 95.1 %all-gather.6.cloned.1.call-start = ((), (), s32[]{:S(2)}) async-start(), calls=%async_computation | async-start | bytes 4325376 | tf_op jit(solution)/shard_map/all_gather | solution.py:68
  8.7 234.9 %all-reduce.4.cloned.1.call-start = ((), (), s32[]{:S(2)}) async-start(), calls=%async_computation.2 | async-start | bytes 8388608 | tf_op jit(solution)/shard_map/psum | solution.py:108
  17.5 3.4 copy-start.4
  17.5 3.4 copy-start.13
  30.1 3.3 copy-start.9
  30.1 3.4 copy-start.12
  30.1 3.5 copy-start.1
  30.1 4.1 copy-start.2
  30.1 4.9 copy-start.3
  150.9 147.5 %all-gather.10.cloned.1.call-start = ((), (), s32[]{:S(2)}) async-start(), calls=%async_computation.3 | async-start | bytes 8650752 | tf_op jit(solution)/shard_map/all_gather | solution.py:117
  151.5 194.9 %all-gather.12.cloned.1.call-start = ((), (), s32[]{:S(2)}) async-start(), calls=%async_computation.4 | async-start | bytes 4325376 | tf_op jit(solution)/shard_map/all_gather | solution.py:126
  152.1 96.5 %copy-start.10 = (f32[2048]{0:T(1024)S(1)}, f32[2048]{0:T(1024)}, u32[]{:S(2)}) copy-start(f32[2048]{0:T(1024)} %param.25) | copy-start | bytes 24580
  152.1 298.2 %all-reduce.6.cloned.1.call-start = ((), (), s32[]{:S(2)}) async-start(), calls=%async_computation.5 | async-start | bytes 8388608 | tf_op jit(solution)/shard_map/psum | solution.py:129
  243.6 5.1 copy-start.5
  243.6 5.9 copy-start.6
  298.5 10.3 %copy-start.8 = (bf16[2,512,2048]{2,1,0:T(8,128)(2,1)S(1)}, bf16[2,512,2048]{2,1,0:T(8,128)(2,1)}, u32[]{:S(2)}) copy-start(bf16[2,512,2048]{2,1,0:T(8,128)(2,1)} %fusion.50) | copy-start | bytes 12582916
  357.6 0.7 copy-start.14
  457.3 2.0 copy-start.7
  457.3 2.8 copy-start.11
Sparse Core Ops, SparseCore 0:
  10.3 45.0 all-gather.7
  57.7 45.2 all-gather.5
  151.1 92.4 all-reduce.3
  246.0 52.4 all-gather.9
  300.8 45.5 all-gather.11
  357.8 92.4 all-reduce.5
where the time goes:
time: 624 us
  waiting for transfers between devices  320 us (51%)
  blocking collectives  154 us (25%)
  matrix products  71.7 us (11%)
  local copies, waits for them, and re-layouts  37.1 us (6%)
  other arithmetic  26.4 us (4%)
  between operations  15 us (2%)
    psum x1, waiting for transfers between devices, per_device(): lax.psum(head_part.astype(jnp.bfloat16), 'mlp').astype(jnp.float32)  91.4 us
    psum x1, waiting for transfers between devices, per_device(): lax.psum(unit_part.astype(jnp.bfloat16), 'mlp').astype(jnp.float32)  90.6 us
    unnamed x1, blocking collectives  64.6 us
    pmax x1, blocking collectives, per_device(): slot_peak = lax.pmax(jnp.max(logits, axis=1), ('req', 'mlp'))  64.5 us
    all_gather x1, waiting for transfers between devices, per_device(): lax.all_gather(adapter_down, 'req', axis=0, tiled=True)  45.8 us
    all_gather x1, waiting for transfers between devices, per_device(): shard_piece = lax.all_gather(w_gateup, 'req', axis=0, tiled=True)  45.4 us
    unnamed x35, local copies, waits for them, and re-layouts  25.3 us
    all_gather x1, blocking collectives, per_device(): lax.all_gather(last_normed, 'req', axis=0, tiled=True)  24.8 us
  transfers between devices with their start and end apart: 6, of which 6 were waited for; matrix products, arithmetic and copies ran while one was open for 10% of the time, Pallas kernels for 0%

commit v1 on v0

--- a/solution.py
+++ b/solution.py
@@ -123,7 +123,9 @@
     activated = (jax.nn.silu(gate_up[:, :unit_cols]) * gate_up[:, unit_cols:]).astype(jnp.bfloat16)
     unit_part = jnp.dot(
         activated,
-        lax.all_gather(w_down, "req", axis=1, tiled=True),
+        jnp.concatenate(
+            lax.all_to_all(jnp.stack([w_down] * lax.axis_size("req")), "req", 0, 0), axis=1
+        ),
         preferred_element_type=jnp.float32,
     )
     unit_total = lax.psum(unit_part.astype(jnp.bfloat16), "mlp").astype(jnp.float32)

time: 624 us -> 600 us (0.962)
  waiting for transfers between devices: 320 us -> 287 us
    all_gather x1 -> x0, waiting for transfers between devices: 24.4 us -> none  [per_device(): lax.all_gather(w_down, 'req', axis=1, tiled=True)]
    psum x1, waiting for transfers between devices: 91.4 us -> 83.8 us  [per_device(): lax.psum(head_part.astype(jnp.bfloat16), 'mlp').astype(jnp.float32)]
    unnamed x35 -> x37, local copies, waits for them, and re-layouts: 25.3 us -> 25.6 us
  transfers between devices with their start and end apart: 6 -> 6, of which waited for: 6 -> 5; matrix products, arithmetic and copies ran while one was open for 10% -> 10% of each run, Pallas kernels for 0% -> 0%
where the time goes in v1:
time: 600 us; the launch traced here: 599 us
  waiting for transfers between devices  287 us (48%)
  blocking collectives  154 us (26%)
  matrix products  71.5 us (12%)
  local copies, waits for them, and re-layouts  39.9 us (7%)
  other arithmetic  26.4 us (4%)
  between operations  14.7 us (2%)
    psum x1, waiting for transfers between devices, per_device(): lax.psum(unit_part.astype(jnp.bfloat16), 'mlp').astype(jnp.float32)  90.9 us
    psum x1, waiting for transfers between devices, per_device(): lax.psum(head_part.astype(jnp.bfloat16), 'mlp').astype(jnp.float32)  83.8 us
    unnamed x1, blocking collectives  64.6 us
    pmax x1, blocking collectives, per_device(): slot_peak = lax.pmax(jnp.max(logits, axis=1), ('req', 'mlp'))  64.5 us
    all_gather x1, waiting for transfers between devices, per_device(): lax.all_gather(adapter_down, 'req', axis=0, tiled=True)  45.8 us
    all_gather x1, waiting for transfers between devices, per_device(): shard_piece = lax.all_gather(w_gateup, 'req', axis=0, tiled=True)  45.4 us
    unnamed x37, local copies, waits for them, and re-layouts  25.6 us
    all_gather x1, blocking collectives, per_device(): lax.all_gather(last_normed, 'req', axis=0, tiled=True)  24.8 us
  transfers between devices with their start and end apart: 6, of which 5 were waited for; matrix products, arithmetic and copies ran while one was open for 10% of the time, Pallas kernels for 0%

profile of v1, /device:TPU:0, one launch (start us, length us, event | category | flops | bytes accessed | tf_op | source)
XLA Modules:
  0.0 599.1 jit_solution(15618792226613991463)
XLA Ops:
  7.2 0.7 all-gather.7.cloned.1.call-update
  8.0 0.7 all-gather.5.cloned.1.call-update
  8.7 8.8 %copy.27 = bf16[2048,3,512]{0,2,1:T(8,128)(2,1)} copy(bf16[2048,3,512]{2,0,1:T(8,128)(2,1)} %param.27) | data formatting | bytes 12582912 | tf_op args[8]
  17.5 3.2 fusion.44
  20.8 0.2 copy-done.4
  21.0 9.1 %fusion.53 = f32[2,512,3,512]{1,3,2,0:T(8,128)S(1)} fusion(bf16[2048,3,512]{0,2,1:T(8,128)(2,1)} %copy.27, bf16[2,512,2048]{2,1,0:T(8,128)(2,1)S(1)} %copy-done.4, f32[2048]{0:T(1024)S(1)} %copy-done.14, f32[2,512]{1,0:T(2,128)S(1)} %add_rsqrt_fusion.1), kind=kOutput, calls=%fused_computation.55 | convolution fusion | flops 6450839552 | bytes 16789504 | tf_op jit(solution)/shard_map/dot_general | solution.py:62
  30.1 1.7 slice.51
  31.8 1.6 copy-done.9
  33.3 0.1 slice.74
  33.5 0.1 compare_select_fusion.1
  33.6 0.6 gather_fusion.2
  34.2 0.6 gather_fusion.3
  34.9 0.1 broadcast_add_fusion
  35.0 0.6 gather_fusion.4
  35.6 0.3 fusion.73
  36.0 19.5 %all-gather.7.cloned.1.call-done = bf16[64,16,512]{2,1,0:T(8,128)(2,1)} async-done(((bf16[2,16,512]{2,1,0:T(8,128)(2,1)}), bf16[64,16,512]{2,1,0:T(8,128)(2,1)}) %all-gather.7.cloned.1.call-update) | async-done | bytes 1048592 | tf_op jit(solution)/shard_map/all_gather | solution.py:69
  55.4 1.8 gather_fusion.1
  57.2 45.8 %all-gather.5.cloned.1.call-done = bf16[64,16,2048]{2,1,0:T(8,128)(2,1)} async-done(((bf16[2,16,2048]{2,1,0:T(8,128)(2,1)}), bf16[64,16,2048]{2,1,0:T(8,128)(2,1)}) %all-gather.5.cloned.1.call-update) | async-done | bytes 4194320 | tf_op jit(solution)/shard_map/all_gather | solution.py:68
  103.0 2.7 gather_fusion
  105.8 5.8 fusion.61
  111.6 2.9 subtract_convert_fusion
  114.4 1.5 pad_maximum_fusion
  116.0 28.0 %while.11 = (s32[]{:T(128)}, bf16[2,512,8,64]{1,3,2,0:T(8,128)(2,1)}, bf16[2,512,8,64]{1,3,2,0:T(8,128)(2,1)S(1)}, s32[2]{0:T(128)S(1)}, bf16[2,512,8,64]{1,3,2,...) while((s32[]{:T(128)}, bf16[2,512,8,64]{1,3,2,0:T(8,128)(2,1)}, ...), condition=%wide.region_4.6_spmd.clone, body=%wide.region_1.5_spmd.clone.sunk | while | flops 550241280 | bytes 19434588 | solution.py:104
  116.0 0.6 dynamic_slice.68
  116.6 0.6 iota_compare_fusion.5
  117.2 0.1 fusion.115
  117.3 7.6 %fusion.116 = (f32[8,512]{1,0:T(8,128)S(1)}, f32[8,512,512]{1,2,0:T(8,128)}) fusion(pred[512,512]{0,1:T(8,128)(4,1)S(1)} %fusion.115, bf16[2,512,8,64]{1,3,2,0:T(8,128)(2,1)} %get-tuple-element.155, s32[]{:T(128)} %get-tuple-element.143, bf16[2,512,8,64]{1,3,2,0:T(8,128)(2,1)} %get-tuple-element.154), kind=kOutput, calls=%fused_computation.116.clone.1 | convolution fusion | flops 276824576 | bytes 9716736 | tf_op jit(solution)/shard_map/while/body/eval_jaxpr/sub | solution.py:99
  124.9 5.0 fusion.117
  130.0 0.6 dynamic_slice.68
  130.5 0.6 iota_compare_fusion.5
  131.2 0.1 fusion.115
  131.3 7.6 %fusion.116 = (f32[8,512]{1,0:T(8,128)S(1)}, f32[8,512,512]{1,2,0:T(8,128)}) fusion(pred[512,512]{0,1:T(8,128)(4,1)S(1)} %fusion.115, bf16[2,512,8,64]{1,3,2,0:T(8,128)(2,1)} %get-tuple-element.155, s32[]{:T(128)} %get-tuple-element.143, bf16[2,512,8,64]{1,3,2,0:T(8,128)(2,1)} %get-tuple-element.154), kind=kOutput, calls=%fused_computation.116.clone.1 | convolution fusion | flops 276824576 | bytes 9716736 | tf_op jit(solution)/shard_map/while/body/eval_jaxpr/sub | solution.py:99
  138.9 5.0 fusion.117
  143.9 2.3 copy.28
  146.3 0.2 copy.33
  146.5 4.3 convolution_convert_fusion
  150.9 0.5 all-gather.9.cloned.1.call-update
  151.4 0.3 copy-done.10
  151.7 2.5 stack.2
  154.3 5.4 all-to-all-start
  159.7 83.8 %all-reduce.4.cloned.1.call-done = bf16[2,512,2048]{2,1,0:T(8,128)(2,1)} async-done(((bf16[2,512,2048]{2,1,0:T(8,128)(2,1)}), bf16[2,512,2048]{2,1,0:T(8,128)(2,1)}) %all-reduce.4.cloned.1.call-update) | async-done | bytes 4194320 | tf_op jit(solution)/shard_map/psum | solution.py:108
  243.5 5.0 fusion.48
  248.6 0.9 copy-done.6
  249.4 3.6 fusion.50
  253.0 45.4 %all-gather.9.cloned.1.call-done = bf16[2048,2,1024]{2,1,0:T(2,128)(2,1)} async-done(((bf16[64,2,1024]{2,1,0:T(2,128)(2,1)}), bf16[2048,2,1024]{2,1,0:T(2,128)(2,1)}) %all-gather.9.cloned.1.call-update) | async-done | bytes 8388624 | tf_op jit(solution)/shard_map/all_gather | solution.py:117
  298.4 10.3 %copy.34 = bf16[256,8,2,1024]{3,1,2,0:T(8,128)(2,1)} copy(bf16[256,8,2,1024]{3,2,1,0:T(2,128)(2,1)} %bitcast.103) | data formatting | bytes 16777216
  308.7 13.2 %fusion.97 = f32[1024,2048]{1,0:T(8,128)} fusion(bf16[1024,2048]{1,0:T(8,128)(2,1)S(1)} %bitcast.105, bf16[2048,2048]{1,0:T(8,128)(2,1)} %bitcast.104), kind=kOutput, calls=%fused_computation.117 | convolution fusion | flops 8589934592 | bytes 20971520 | tf_op jit(solution)/shard_map/dot_general | solution.py:118
  321.9 11.2 %convolution_convert_fusion.1 = bf16[1024,2048]{1,0:T(8,128)(2,1)} fusion(bf16[1024,2048]{0,1:T(8,128)(2,1)} %bitcast.13, f32[1024,2048]{1,0:T(8,128)} %fusion.97), kind=kOutput, calls=%fused_computation.61 | convolution fusion | flops 4303355904 | bytes 16777216 | tf_op jit(solution)/shard_map/dot_general | solution.py:124
  333.1 0.6 copy-done.15
  333.8 0.6 dynamic-slice
  335.0 0.1 iota_compare_fusion.3
  335.1 90.9 %all-reduce.6.cloned.1.call-done = bf16[2,512,2048]{2,1,0:T(8,128)(2,1)} async-done(((bf16[2,512,2048]{2,1,0:T(8,128)(2,1)}), bf16[2,512,2048]{2,1,0:T(8,128)(2,1)}) %all-reduce.6.cloned.1.call-update) | async-done | bytes 4194320 | tf_op jit(solution)/shard_map/psum | solution.py:131
  426.0 6.9 %multiply_reduce_fusion = (f32[2]{0:T(128)S(1)}, bf16[2,512,2048]{2,1,0:T(8,128)(2,1)S(1)}) fusion(bf16[2,512,2048]{2,1,0:T(8,128)(2,1)} %all-reduce.6.cloned.1.call-done, bf16[2,512,2048]{2,1,0:T(8,128)(2,1)} %all-reduce.4.cloned.1.call-done, bf16[2,512,2048]{2,1,0:T(8,128)(2,1)} %param.19, pred[2,512]{1,0:T(4,128)(4,1)S(1)} %iota_compare_fusion.3), kind=kLoop, calls=%fused_computation.54 | loop fusion | flops 25165822 | bytes 16778248 | tf_op jit(solution)/shard_map/reduce_sum | solution.py:136
  433.0 2.0 copy-done.7
  435.0 0.7 fusion.82
  435.6 0.1 fusion.78
  435.8 0.1 fusion.80
  435.9 24.8 %all-gather = bf16[32,2,2048]{2,1,0:T(2,128)(2,1)S(1)} all-gather(bf16[1,2,2048]{2,1,0:T(2,128)(2,1)S(1)} %bitcast.112), channel_id=1, replica_groups=mesh['req'=32,'mlp'=4] {'req'}, dimensions={0}, use_global_device_ids=true | all-gather | bytes 270336 | tf_op jit(solution)/shard_map/all_gather | solution.py:143
  460.6 0.1 reshape.240
  460.7 2.1 convolution_reduce_fusion
  462.8 64.5 %pmax.7 = f32[64]{0:T(128)S(1)} all-reduce(f32[64]{0:T(128)S(1)} %convolution_reduce_fusion), channel_id=1, replica_groups=mesh['req'=32,'mlp'=4] {'req','mlp'}, use_global_device_ids=true, to_apply=%region_12.14 | all-reduce | flops 64 | bytes 512 | tf_op jit(solution)/shard_map/pmax | solution.py:152
  527.3 0.1 sqrt_dynamic-update-slice_fusion
  527.4 64.6 %all-reduce = f32[64]{0:T(128)S(1)} all-reduce(f32[64]{0:T(128)S(1)} %sqrt_dynamic-update-slice_fusion), channel_id=1, replica_groups=mesh['req'=32,'mlp'=4] {'req'}, use_global_device_ids=true, to_apply=%add | all-reduce | flops 64 | bytes 512
  592.0 0.6 select_reduce_fusion
  (45 shorter events, 0.5 us)
Async XLA Ops:
  7.2 139.3 %copy-start = (bf16[512,2048]{1,0:T(8,128)(2,1)S(1)}, bf16[512,2048]{1,0:T(8,128)(2,1)}, u32[]{:S(2)}) copy-start(bf16[512,2048]{1,0:T(8,128)(2,1)} %param.28) | copy-start | bytes 6291460
  7.2 48.2 %all-gather.7.cloned.1.call-start = ((), (), s32[]{:S(2)}) async-start(), calls=%async_computation.2 | async-start | bytes 1081344 | tf_op jit(solution)/shard_map/all_gather | solution.py:69
  7.9 95.1 %all-gather.5.cloned.1.call-start = ((), (), s32[]{:S(2)}) async-start(), calls=%async_computation.1 | async-start | bytes 4325376 | tf_op jit(solution)/shard_map/all_gather | solution.py:68
  8.7 234.9 %all-reduce.4.cloned.1.call-start = ((), (), s32[]{:S(2)}) async-start(), calls=%async_computation.3 | async-start | bytes 8388608 | tf_op jit(solution)/shard_map/psum | solution.py:108
  17.5 3.4 copy-start.4
  17.5 3.4 copy-start.14
  30.1 3.3 copy-start.9
  30.1 3.4 copy-start.13
  30.1 3.5 copy-start.1
  30.1 4.1 copy-start.2
  30.1 4.9 copy-start.3
  150.8 0.9 copy-start.10
  150.9 147.5 %all-gather.9.cloned.1.call-start = ((), (), s32[]{:S(2)}) async-start(), calls=%async_computation.4 | async-start | bytes 8650752 | tf_op jit(solution)/shard_map/all_gather | solution.py:117
  154.3 167.6 %all-to-all-start = ((bf16[32,1024,64]{1,2,0:T(8,128)(2,1)}), bf16[32,1024,64]{1,2,0:T(8,128)(2,1)}, u32[]{:S(2)}, u32[]{:S(2)}) async-start(bf16[32,1024,64]{1,2,0:T(8,128)(2,1)} %stack.2), calls=%async_computation | async-start | bytes 8388608 | tf_op jit(solution)/shard_map/all_to_all | solution.py:127
  159.7 88.9 %copy-start.11 = (f32[2048]{0:T(1024)S(1)}, f32[2048]{0:T(1024)}, u32[]{:S(2)}) copy-start(f32[2048]{0:T(1024)} %param.25) | copy-start | bytes 24580
  159.7 266.3 %all-reduce.6.cloned.1.call-start = ((), (), s32[]{:S(2)}) async-start(), calls=%async_computation.5 | async-start | bytes 8388608 | tf_op jit(solution)/shard_map/psum | solution.py:131
  243.5 5.1 copy-start.5
  243.5 5.9 copy-start.6
  298.4 10.3 %copy-start.8 = (bf16[2,512,2048]{2,1,0:T(8,128)(2,1)S(1)}, bf16[2,512,2048]{2,1,0:T(8,128)(2,1)}, u32[]{:S(2)}) copy-start(bf16[2,512,2048]{2,1,0:T(8,128)(2,1)} %fusion.50) | copy-start | bytes 12582916
  333.1 0.7 copy-start.15
  432.9 2.0 copy-start.7
  432.9 2.8 copy-start.12
Sparse Core Ops, SparseCore 0:
  10.3 45.0 all-gather.6
  57.7 45.2 all-gather.4
  151.0 92.4 all-reduce.3
  245.9 52.4 all-gather.8
  333.2 92.7 all-reduce.5
